TPU v7x, 32 devices: a whole 2x2x4 slice. The times are simulated.
32 devices in a mesh: grp: 4 (over z), dev: 8 (over y, x, core).
Axes of the slice: x: 2, y: 2, z: 4, core: 2. Of those that a mesh axis runs over, the one named last changes fastest.
Arguments:
- matrix: float32 [65536, 1024], P(('grp', 'dev')), may hold values from -60 to 60
- block_order: int32 [4, 128], P('grp'), may hold values from 0 to 127, as said below
- counts: int32 [4, 8], P('grp'), may hold values from 0 to 32, as said below
- sign_bits: int32 [4, 128, 128], P('grp'), may hold values from 0 to 1
- row_mask: int32 [4, 128, 128], P('grp'), may hold values from 0 to 1, as said below
Outputs:
- sketch: float32 [32768, 1024], P(('grp', 'dev'))
- group_factor: float32 [4, 1024, 1024], P('grp', 'dev')
- factor: float32 [1024, 1024], P('dev')
Inputs may be any that keep to these rules, and one draw needn't show every extreme that they name: Each row of block_order is a permutation of the group's block indices; at most 4 blocks of one device's blocks are placed in the positions held by one device, and some pair reaches 4. `counts`: each row sums to 128; its largest entry is exactly 32. `row_mask`: exactly 32 ones in each row of 128.
All inputs are finite; a program needn't handle non-finite values.
Results may differ from a plain program's by a relative error of at most 0.0003.
Values sent between devices are 32-bit elements; how exact they have to be, the bound alone decides.
No kernel may reach another device: no remote copies, remote signals or barrier semaphores. Data moves between devices by JAX's collectives and lax.ppermute only.
A program may use at most 128 MiB of HBM per device.

v0:
```python
import jax
import jax.numpy as jnp
from jax import lax
from jax.sharding import PartitionSpec as P

BLOCK = 128
KEEP = 32


def hadamard(order_of):
    indices = jnp.arange(order_of, dtype=jnp.int32)
    common = jnp.bitwise_and(indices[:, None], indices[None, :])
    parity = jnp.zeros_like(common)
    for shift_by in range(order_of.bit_length() - 1):
        parity = parity + jnp.bitwise_and(jnp.right_shift(common, shift_by), 1)
    return (1 - 2 * (parity % 2)).astype(jnp.float32)


def mix_blocks(block_list, mask_rows, sign_rows, walsh_sign_matrix):
    running = jnp.cumsum(mask_rows, axis=1) - 1
    choose_row = jnp.arange(KEEP, dtype=jnp.int32)[None, :, None]
    select_rows = ((mask_rows[:, None, :] == 1) & (running[:, None, :] == choose_row)).astype(
        jnp.float32
    )
    mixing_transform = jnp.einsum(
        "jlf,fp->jlp", select_rows, walsh_sign_matrix, precision=lax.Precision.HIGHEST
    )
    mixing_transform = mixing_transform * (1 - 2 * sign_rows).astype(jnp.float32)[:, None, :]
    normalize_rows = float(walsh_sign_matrix.shape[0]) ** (-0.5)
    return (
        jnp.einsum("uwd,udk->uwk", mixing_transform, block_list, precision=lax.Precision.HIGHEST)
        * normalize_rows
    )


def gram_of(mixed_rows):
    flat_rows = mixed_rows.reshape(-1, mixed_rows.shape[-1])
    return jnp.einsum("kc,ke->ce", flat_rows, flat_rows, precision=lax.Precision.HIGHEST)


def body(matrix, block_order, counts, sign_bits, row_mask):
    blocks_dev = matrix.shape[0] // BLOCK
    columns = matrix.shape[1]
    devices = lax.axis_size("dev")
    groups = lax.axis_size("grp")
    me_dev = lax.axis_index("dev")
    positions = devices * blocks_dev
    most_held = 2 * blocks_dev
    capacity = max(1, 2 * blocks_dev // devices)
    order_row = block_order[0]
    count_row = counts[0]
    sign_table = sign_bits[0]
    mask_table = row_mask[0]
    run_ends = jnp.cumsum(count_row)
    offsets = run_ends - count_row
    block_locations = jnp.arange(positions, dtype=jnp.int32)
    owners = jnp.sum((block_locations[:, None] >= run_ends[None, :]).astype(jnp.int32), axis=1)
    source = order_row // blocks_dev
    earlier = (
        (block_locations[None, :] < block_locations[:, None])
        & (owners[None, :] == owners[:, None])
        & (source[None, :] == source[:, None])
    )
    slot_of = jnp.sum(earlier.astype(jnp.int32), axis=1)
    target = owners * capacity + slot_of
    inverse = jnp.zeros((positions,), jnp.int32).at[order_row].set(block_locations)
    my_places = lax.dynamic_slice_in_dim(inverse, me_dev * blocks_dev, blocks_dev)
    my_target = target[my_places]
    buffer_slots = jnp.arange(devices * capacity, dtype=jnp.int32)
    matches = my_target[None, :] == buffer_slots[:, None]
    filled = jnp.any(matches, axis=1)
    pick_block = jnp.sum(
        matches.astype(jnp.int32) * jnp.arange(blocks_dev, dtype=jnp.int32)[None, :], axis=1
    )
    held_slots = jnp.arange(most_held, dtype=jnp.int32)
    my_count = lax.dynamic_index_in_dim(count_row, me_dev, 0, False)
    my_offset = lax.dynamic_index_in_dim(offsets, me_dev, 0, False)
    live_slot = held_slots < my_count
    my_positions = jnp.minimum(my_offset + held_slots, positions - 1)
    from_slot = source[my_positions] * capacity + slot_of[my_positions]
    local_blocks = matrix.reshape(blocks_dev, BLOCK, columns)
    walsh_sign_matrix = hadamard(BLOCK)
    mixed_rows = mix_blocks(
        local_blocks, mask_table[my_places], sign_table[my_places], walsh_sign_matrix
    )
    partial_value = gram_of(mixed_rows)
    outgoing = jnp.where(filled[:, None, None], jnp.take(mixed_rows, pick_block, axis=0), 0.0)
    arrived = lax.all_to_all(outgoing, "dev", split_axis=0, concat_axis=0, tiled=True)
    sketch = jnp.where(live_slot[:, None, None], jnp.take(arrived, from_slot, axis=0), 0.0)
    group_gram = lax.psum(partial_value, "dev") / float(positions * KEEP)
    mean_gram = lax.psum(group_gram, "grp") / float(groups)
    rows_dev = columns // devices
    group_upper = jnp.linalg.cholesky(group_gram).T
    mean_upper = jnp.linalg.cholesky(mean_gram).T
    group_factor = lax.dynamic_slice_in_dim(group_upper, me_dev * rows_dev, rows_dev, 0)[None]
    factor = lax.dynamic_slice_in_dim(mean_upper, me_dev * rows_dev, rows_dev, 0)
    return (sketch.reshape(most_held * KEEP, columns), group_factor, factor)


def solution(mesh):
    placed = (
        P(("grp", "dev"), None),
        P("grp", None),
        P("grp", None),
        P("grp", None, None),
        P("grp", None, None),
    )
    return jax.shard_map(
        body,
        mesh=mesh,
        in_specs=placed,
        out_specs=(P(("grp", "dev"), None), P("grp", "dev", None), P("dev", None)),
        check_vma=False,
    )
```

profile of v0, /device:TPU:0, one launch (start us, length us, event | category | flops | bytes accessed | tf_op | source)
XLA Modules:
  0.0 602.9 jit_solution(12430598933679036047)
XLA Ops:
  46.7 94.5 %all-reduce.4.cloned.1.call-done = f32[1024,1024]{0,1:T(8,128)} async-done(((f32[1024,1024]{0,1:T(8,128)}), f32[1024,1024]{0,1:T(8,128)}) %all-reduce.4.cloned.1.call-update) | async-done | bytes 4194320 | tf_op jit(solution)/shard_map/psum | solution.py:90
  158.7 11.7 %cholesky.619 = f32[128,128]{1,0:T(8,128)S(1)} custom-call(f32[128,128]{1,0:T(8,128)S(1)} %cholesky.911), custom_call_target="Cholesky" | custom-call | tf_op jit(solution)/shard_map/jit(cholesky)/cholesky | solution.py:93
  170.4 9.8 %custom-call.51 = f32[1,128,128]{1,2,0:T(8,128)S(1)} custom-call(f32[1,128,128]{2,1,0:T(8,128)S(1)} %get-tuple-element.58), custom_call_target="InvertDiagBlocksLowerTriangular" | custom-call | tf_op jit(solution)/shard_map/jit(cholesky)/cholesky | solution.py:93
  186.6 11.9 %cholesky.638 = f32[128,128]{1,0:T(8,128)S(1)} custom-call(f32[128,128]{1,0:T(8,128)S(1)} %cholesky.915), custom_call_target="Cholesky" | custom-call | tf_op jit(solution)/shard_map/jit(cholesky)/cholesky | solution.py:93
  199.2 9.8 %custom-call.52 = f32[1,128,128]{1,2,0:T(8,128)S(1)} custom-call(f32[1,128,128]{2,1,0:T(8,128)S(1)} %get-tuple-element.55), custom_call_target="InvertDiagBlocksLowerTriangular" | custom-call | tf_op jit(solution)/shard_map/jit(cholesky)/cholesky | solution.py:93
  212.3 11.7 %cholesky.659 = f32[128,128]{1,0:T(8,128)S(1)} custom-call(f32[128,128]{1,0:T(8,128)S(1)} %cholesky.920), custom_call_target="Cholesky" | custom-call | tf_op jit(solution)/shard_map/jit(cholesky)/cholesky | solution.py:93
  224.7 9.8 %custom-call.53 = f32[1,128,128]{1,2,0:T(8,128)S(1)} custom-call(f32[1,128,128]{2,1,0:T(8,128)S(1)} %get-tuple-element.52), custom_call_target="InvertDiagBlocksLowerTriangular" | custom-call | tf_op jit(solution)/shard_map/jit(cholesky)/cholesky | solution.py:93
  238.1 12.1 %cholesky.678 = f32[128,128]{1,0:T(8,128)S(1)} custom-call(f32[128,128]{1,0:T(8,128)S(1)} %cholesky.925), custom_call_target="Cholesky" | custom-call | tf_op jit(solution)/shard_map/jit(cholesky)/cholesky | solution.py:93
  250.9 9.8 %custom-call.54 = f32[1,128,128]{1,2,0:T(8,128)S(1)} custom-call(f32[1,128,128]{2,1,0:T(8,128)S(1)} %get-tuple-element.49), custom_call_target="InvertDiagBlocksLowerTriangular" | custom-call | tf_op jit(solution)/shard_map/jit(cholesky)/cholesky | solution.py:93
  264.2 11.7 %cholesky.697 = f32[128,128]{1,0:T(8,128)S(1)} custom-call(f32[128,128]{1,0:T(8,128)S(1)} %cholesky.930), custom_call_target="Cholesky" | custom-call | tf_op jit(solution)/shard_map/jit(cholesky)/cholesky | solution.py:93
  276.5 9.9 %custom-call.55 = f32[1,128,128]{1,2,0:T(8,128)S(1)} custom-call(f32[1,128,128]{2,1,0:T(8,128)S(1)} %get-tuple-element.46), custom_call_target="InvertDiagBlocksLowerTriangular" | custom-call | tf_op jit(solution)/shard_map/jit(cholesky)/cholesky | solution.py:93
  289.8 11.7 %cholesky.716 = f32[128,128]{1,0:T(8,128)S(1)} custom-call(f32[128,128]{1,0:T(8,128)S(1)} %cholesky.935), custom_call_target="Cholesky" | custom-call | tf_op jit(solution)/shard_map/jit(cholesky)/cholesky | solution.py:93
  302.1 9.8 %custom-call.56 = f32[1,128,128]{1,2,0:T(8,128)S(1)} custom-call(f32[1,128,128]{2,1,0:T(8,128)S(1)} %get-tuple-element.43), custom_call_target="InvertDiagBlocksLowerTriangular" | custom-call | tf_op jit(solution)/shard_map/jit(cholesky)/cholesky | solution.py:93
  315.0 11.9 %cholesky.735 = f32[128,128]{1,0:T(8,128)S(1)} custom-call(f32[128,128]{1,0:T(8,128)S(1)} %cholesky.940), custom_call_target="Cholesky" | custom-call | tf_op jit(solution)/shard_map/jit(cholesky)/cholesky | solution.py:93
  340.0 11.7 %cholesky.752 = f32[128,128]{1,0:T(8,128)S(1)} custom-call(f32[128,128]{1,0:T(8,128)S(1)} %convolution_subtract_fusion.13), custom_call_target="Cholesky" | custom-call | tf_op jit(solution)/shard_map/jit(cholesky)/cholesky | solution.py:93
  388.9 11.7 %cholesky.767 = f32[128,128]{1,0:T(8,128)S(1)} custom-call(f32[128,128]{1,0:T(8,128)S(1)} %cholesky.945), custom_call_target="Cholesky" | custom-call | tf_op jit(solution)/shard_map/jit(cholesky)/cholesky | solution.py:94
  416.9 11.9 %cholesky.786 = f32[128,128]{1,0:T(8,128)S(1)} custom-call(f32[128,128]{1,0:T(8,128)S(1)} %cholesky.949), custom_call_target="Cholesky" | custom-call | tf_op jit(solution)/shard_map/jit(cholesky)/cholesky | solution.py:94
  443.9 11.7 %cholesky.807 = f32[128,128]{1,0:T(8,128)S(1)} custom-call(f32[128,128]{1,0:T(8,128)S(1)} %cholesky.954), custom_call_target="Cholesky" | custom-call | tf_op jit(solution)/shard_map/jit(cholesky)/cholesky | solution.py:94
  470.2 11.9 %cholesky.826 = f32[128,128]{1,0:T(8,128)S(1)} custom-call(f32[128,128]{1,0:T(8,128)S(1)} %cholesky.959), custom_call_target="Cholesky" | custom-call | tf_op jit(solution)/shard_map/jit(cholesky)/cholesky | solution.py:94
  496.6 11.7 %cholesky.845 = f32[128,128]{1,0:T(8,128)S(1)} custom-call(f32[128,128]{1,0:T(8,128)S(1)} %cholesky.964), custom_call_target="Cholesky" | custom-call | tf_op jit(solution)/shard_map/jit(cholesky)/cholesky | solution.py:94
  509.6 10.2 %custom-call.62 = f32[1,128,128]{1,2,0:T(8,128)S(1)} custom-call(f32[1,128,128]{2,1,0:T(8,128)S(1)} %get-tuple-element.24), custom_call_target="InvertDiagBlocksLowerTriangular" | custom-call | tf_op jit(solution)/shard_map/jit(cholesky)/cholesky | solution.py:94
  523.2 11.7 %cholesky.864 = f32[128,128]{1,0:T(8,128)S(1)} custom-call(f32[128,128]{1,0:T(8,128)S(1)} %cholesky.969), custom_call_target="Cholesky" | custom-call | tf_op jit(solution)/shard_map/jit(cholesky)/cholesky | solution.py:94
  549.0 11.9 %cholesky.883 = f32[128,128]{1,0:T(8,128)S(1)} custom-call(f32[128,128]{1,0:T(8,128)S(1)} %cholesky.974), custom_call_target="Cholesky" | custom-call | tf_op jit(solution)/shard_map/jit(cholesky)/cholesky | solution.py:94
  574.5 11.7 %cholesky.900 = f32[128,128]{1,0:T(8,128)S(1)} custom-call(f32[128,128]{1,0:T(8,128)S(1)} %convolution_subtract_fusion.12), custom_call_target="Cholesky" | custom-call | tf_op jit(solution)/shard_map/jit(cholesky)/cholesky | solution.py:94
  (155 shorter events, 225.8 us)
Async XLA Ops:
  7.2 1.8 copy-start
  7.2 134.0 %all-reduce.4.cloned.1.call-start = ((), (), s32[]{:S(2)}) async-start(), calls=%async_computation.1 | async-start | bytes 8388608 | tf_op jit(solution)/shard_map/psum | solution.py:90
  26.7 0.7 copy-start.4
  26.7 0.7 copy-start.5
  40.2 322.5 %all-to-all-start = ((f32[32,32,1024]{2,1,0:T(8,128)}), f32[32,32,1024]{2,1,0:T(8,128)}, u32[]{:S(2)}, u32[]{:S(2)}) async-start(f32[32,32,1024]{2,1,0:T(8,128)} %select_select_fusion), calls=%async_computation | async-start | bytes 8388608 | tf_op jit(solution)/shard_map/all_to_all | solution.py:88
  151.5 220.3 %all-reduce.6.cloned.1.call-start = ((), (), s32[]{:S(2)}) async-start(), calls=%async_computation.2 | async-start | bytes 8388608 | tf_op jit(solution)/shard_map/psum | solution.py:91
  156.7 2.0 copy-start.3
  387.0 1.9 copy-start.2
  520.9 75.0 %copy-start.1 = (s32[1,128,128]{2,1,0:T(8,128)S(1)}, s32[1,128,128]{2,1,0:T(8,128)}, u32[]{:S(2)}) copy-start(s32[1,128,128]{2,1,0:T(8,128)} %param.10) | copy-start | bytes 196612
Sparse Core Ops, SparseCore 0:
  26.9 114.2 all-reduce.3
  154.7 155.1 all-reduce.5
where the time goes:
time: 611 us; the launch traced here: 603 us
  other arithmetic  379 us (62%)
  waiting for transfers between devices  95 us (16%)
  matrix products  61.8 us (10%)
  local copies, waits for them, and re-layouts  36.9 us (6%)
  between operations  24.9 us (4%)
    another operation x31, other arithmetic, body(): group_upper = jnp.linalg.cholesky(group_gram).T  173 us
    another operation x31, other arithmetic, body(): mean_upper = jnp.linalg.cholesky(mean_gram).T  173 us
    psum x1, waiting for transfers between devices, body(): group_gram = lax.psum(partial_value, 'dev') / float(positions * KEEP)  94.5 us
    another operation x14, matrix products, body(): group_upper = jnp.linalg.cholesky(group_gram).T  23.2 us
    another operation x14, matrix products, body(): mean_upper = jnp.linalg.cholesky(mean_gram).T  23.1 us
  transfers between devices with their start and end apart: 3, of which 1 were waited for; matrix products, arithmetic and copies ran while one was open for 39% of the time, Pallas kernels for 0%

commit v1 on v0

--- a/solution.py
+++ b/solution.py
@@ -87,7 +87,7 @@
     outgoing = jnp.where(filled[:, None, None], jnp.take(mixed_rows, pick_block, axis=0), 0.0)
     arrived = lax.all_to_all(outgoing, "dev", split_axis=0, concat_axis=0, tiled=True)
     sketch = jnp.where(live_slot[:, None, None], jnp.take(arrived, from_slot, axis=0), 0.0)
-    group_gram = lax.psum(partial_value, "dev") / float(positions * KEEP)
+    group_gram = jnp.sum(lax.all_gather(partial_value, "dev"), axis=0) / float(positions * KEEP)
     mean_gram = lax.psum(group_gram, "grp") / float(groups)
     rows_dev = columns // devices
     group_upper = jnp.linalg.cholesky(group_gram).T

time: 611 us -> 723 us (1.18)
  waiting for transfers between devices: 95 us -> 177 us
  other arithmetic: 379 us -> 404 us
    psum x1 -> x0, waiting for transfers between devices: 94.5 us -> none  [body(): group_gram = lax.psum(partial_value, 'dev') / float(positions * KEEP)]
    all_gather x0 -> x1, waiting for transfers between devices: none -> 90.1 us  [body(): lax.all_gather(partial_value, 'dev')]
    all_to_all x1, waiting for transfers between devices: 0.01 us -> 86.7 us  [body(): lax.all_to_all(outgoing, 'dev', split_axis=0, concat_axis=0, tiled=True)]
    reduce_sum x0 -> x1, other arithmetic: none -> 14.7 us  [body(): jnp.sum(lax.all_gather(partial_value, 'dev'), axis=0)]
    another operation x31, other arithmetic: 173 us -> 181 us  [body(): group_upper = jnp.linalg.cholesky(group_gram).T]
  transfers between devices with their start and end apart: 3 -> 3, of which waited for: 1 -> 2; matrix products, arithmetic and copies ran while one was open for 39% -> 30% of each run, Pallas kernels for 0% -> 0%
where the time goes in v1:
time: 723 us; the launch traced here: 716 us
  other arithmetic  404 us (56%)
  waiting for transfers between devices  177 us (24%)
  matrix products  61.7 us (9%)
  local copies, waits for them, and re-layouts  42.1 us (6%)
  between operations  25.1 us (3%)
    another operation x31, other arithmetic, body(): group_upper = jnp.linalg.cholesky(group_gram).T  181 us
    another operation x31, other arithmetic, body(): mean_upper = jnp.linalg.cholesky(mean_gram).T  173 us
    all_gather x1, waiting for transfers between devices, body(): lax.all_gather(partial_value, 'dev')  90.1 us
    all_to_all x1, waiting for transfers between devices, body(): lax.all_to_all(outgoing, 'dev', split_axis=0, concat_axis=0, tiled=True)  86.7 us
    another operation x14, matrix products, body(): group_upper = jnp.linalg.cholesky(group_gram).T  23.2 us
    another operation x14, matrix products, body(): mean_upper = jnp.linalg.cholesky(mean_gram).T  23.1 us
    reduce_sum x1, other arithmetic, body(): jnp.sum(lax.all_gather(partial_value, 'dev'), axis=0)  14.7 us
  transfers between devices with their start and end apart: 3, of which 2 were waited for; matrix products, arithmetic and copies ran while one was open for 30% of the time, Pallas kernels for 0%

profile of v1, /device:TPU:0, one launch (start us, length us, event | category | flops | bytes accessed | tf_op | source)
XLA Modules:
  0.0 715.7 jit_solution(11078389760128059456)
XLA Ops:
  48.0 86.7 %all-to-all-done = f32[32,32,1024]{2,1,0:T(8,128)} async-done(((f32[32,32,1024]{2,1,0:T(8,128)}), f32[32,32,1024]{2,1,0:T(8,128)}, u32[]{:S(2)}, u32[]{:S(2)}) %all-to-all-start) | async-done | bytes 4194336 | tf_op jit(solution)/shard_map/all_to_all | solution.py:88
  145.2 90.1 %all-gather.3.cloned.1.call-done = f32[8192,1024]{1,0:T(8,128)} async-done(((f32[1024,1024]{1,0:T(8,128)}), f32[8192,1024]{1,0:T(8,128)}) %all-gather.3.cloned.1.call-update) | async-done | bytes 33554448 | tf_op jit(solution)/shard_map/all_gather | solution.py:90
  235.2 14.7 %reduce_sum.42 = f32[1024,1024]{1,0:T(8,128)} reduce(f32[8,1024,1024]{2,1,0:T(8,128)} %bitcast.139, f32[]{:T(128)} %constant.301.clone.1), dimensions={0}, to_apply=%region_7.8 | reduce | flops 7340032 | bytes 37748740 | tf_op jit(solution)/shard_map/reduce_sum | solution.py:90
  272.0 11.7 %cholesky.619 = f32[128,128]{1,0:T(8,128)S(1)} custom-call(f32[128,128]{1,0:T(8,128)S(1)} %cholesky.911), custom_call_target="Cholesky" | custom-call | tf_op jit(solution)/shard_map/jit(cholesky)/cholesky | solution.py:93
  286.3 9.8 %custom-call.51 = f32[1,128,128]{1,2,0:T(8,128)S(1)} custom-call(f32[1,128,128]{2,1,0:T(8,128)S(1)} %get-tuple-element.61), custom_call_target="InvertDiagBlocksLowerTriangular" | custom-call | tf_op jit(solution)/shard_map/jit(cholesky)/cholesky | solution.py:93
  300.0 20.4 %cholesky.638 = f32[128,128]{1,0:T(8,128)S(1)} custom-call(f32[128,128]{1,0:T(8,128)S(1)} %cholesky.915), custom_call_target="Cholesky" | custom-call | tf_op jit(solution)/shard_map/jit(cholesky)/cholesky | solution.py:93
  334.3 11.7 %cholesky.659 = f32[128,128]{1,0:T(8,128)S(1)} custom-call(f32[128,128]{1,0:T(8,128)S(1)} %cholesky.920), custom_call_target="Cholesky" | custom-call | tf_op jit(solution)/shard_map/jit(cholesky)/cholesky | solution.py:93
  360.0 11.9 %cholesky.678 = f32[128,128]{1,0:T(8,128)S(1)} custom-call(f32[128,128]{1,0:T(8,128)S(1)} %cholesky.925), custom_call_target="Cholesky" | custom-call | tf_op jit(solution)/shard_map/jit(cholesky)/cholesky | solution.py:93
  372.6 9.8 %custom-call.54 = f32[1,128,128]{1,2,0:T(8,128)S(1)} custom-call(f32[1,128,128]{2,1,0:T(8,128)S(1)} %get-tuple-element.52), custom_call_target="InvertDiagBlocksLowerTriangular" | custom-call | tf_op jit(solution)/shard_map/jit(cholesky)/cholesky | solution.py:93
  385.8 11.7 %cholesky.697 = f32[128,128]{1,0:T(8,128)S(1)} custom-call(f32[128,128]{1,0:T(8,128)S(1)} %cholesky.930), custom_call_target="Cholesky" | custom-call | tf_op jit(solution)/shard_map/jit(cholesky)/cholesky | solution.py:93
  398.2 10.2 %custom-call.55 = f32[1,128,128]{1,2,0:T(8,128)S(1)} custom-call(f32[1,128,128]{2,1,0:T(8,128)S(1)} %get-tuple-element.49), custom_call_target="InvertDiagBlocksLowerTriangular" | custom-call | tf_op jit(solution)/shard_map/jit(cholesky)/cholesky | solution.py:93
  411.7 11.7 %cholesky.716 = f32[128,128]{1,0:T(8,128)S(1)} custom-call(f32[128,128]{1,0:T(8,128)S(1)} %cholesky.935), custom_call_target="Cholesky" | custom-call | tf_op jit(solution)/shard_map/jit(cholesky)/cholesky | solution.py:93
  424.1 9.8 %custom-call.56 = f32[1,128,128]{1,2,0:T(8,128)S(1)} custom-call(f32[1,128,128]{2,1,0:T(8,128)S(1)} %get-tuple-element.46), custom_call_target="InvertDiagBlocksLowerTriangular" | custom-call | tf_op jit(solution)/shard_map/jit(cholesky)/cholesky | solution.py:93
  436.9 11.9 %cholesky.735 = f32[128,128]{1,0:T(8,128)S(1)} custom-call(f32[128,128]{1,0:T(8,128)S(1)} %cholesky.940), custom_call_target="Cholesky" | custom-call | tf_op jit(solution)/shard_map/jit(cholesky)/cholesky | solution.py:93
  461.8 11.7 %cholesky.752 = f32[128,128]{1,0:T(8,128)S(1)} custom-call(f32[128,128]{1,0:T(8,128)S(1)} %convolution_subtract_fusion.13), custom_call_target="Cholesky" | custom-call | tf_op jit(solution)/shard_map/jit(cholesky)/cholesky | solution.py:93
  501.4 11.7 %cholesky.767 = f32[128,128]{1,0:T(8,128)S(1)} custom-call(f32[128,128]{1,0:T(8,128)S(1)} %cholesky.945), custom_call_target="Cholesky" | custom-call | tf_op jit(solution)/shard_map/jit(cholesky)/cholesky | solution.py:94
  529.4 12.1 %cholesky.786 = f32[128,128]{1,0:T(8,128)S(1)} custom-call(f32[128,128]{1,0:T(8,128)S(1)} %cholesky.949), custom_call_target="Cholesky" | custom-call | tf_op jit(solution)/shard_map/jit(cholesky)/cholesky | solution.py:94
  556.6 11.7 %cholesky.807 = f32[128,128]{1,0:T(8,128)S(1)} custom-call(f32[128,128]{1,0:T(8,128)S(1)} %cholesky.954), custom_call_target="Cholesky" | custom-call | tf_op jit(solution)/shard_map/jit(cholesky)/cholesky | solution.py:94
  582.9 11.9 %cholesky.826 = f32[128,128]{1,0:T(8,128)S(1)} custom-call(f32[128,128]{1,0:T(8,128)S(1)} %cholesky.959), custom_call_target="Cholesky" | custom-call | tf_op jit(solution)/shard_map/jit(cholesky)/cholesky | solution.py:94
  609.3 11.7 %cholesky.845 = f32[128,128]{1,0:T(8,128)S(1)} custom-call(f32[128,128]{1,0:T(8,128)S(1)} %cholesky.964), custom_call_target="Cholesky" | custom-call | tf_op jit(solution)/shard_map/jit(cholesky)/cholesky | solution.py:94
  622.3 10.0 %custom-call.62 = f32[1,128,128]{1,2,0:T(8,128)S(1)} custom-call(f32[1,128,128]{2,1,0:T(8,128)S(1)} %get-tuple-element.27), custom_call_target="InvertDiagBlocksLowerTriangular" | custom-call | tf_op jit(solution)/shard_map/jit(cholesky)/cholesky | solution.py:94
  635.7 11.7 %cholesky.864 = f32[128,128]{1,0:T(8,128)S(1)} custom-call(f32[128,128]{1,0:T(8,128)S(1)} %cholesky.969), custom_call_target="Cholesky" | custom-call | tf_op jit(solution)/shard_map/jit(cholesky)/cholesky | solution.py:94
  661.5 11.9 %cholesky.883 = f32[128,128]{1,0:T(8,128)S(1)} custom-call(f32[128,128]{1,0:T(8,128)S(1)} %cholesky.974), custom_call_target="Cholesky" | custom-call | tf_op jit(solution)/shard_map/jit(cholesky)/cholesky | solution.py:94
  687.1 11.7 %cholesky.900 = f32[128,128]{1,0:T(8,128)S(1)} custom-call(f32[128,128]{1,0:T(8,128)S(1)} %convolution_subtract_fusion.12), custom_call_target="Cholesky" | custom-call | tf_op jit(solution)/shard_map/jit(cholesky)/cholesky | solution.py:94
  (157 shorter events, 252.4 us)
Async XLA Ops:
  7.2 1.8 copy-start
  7.2 228.0 %all-gather.3.cloned.1.call-start = ((), (), s32[]{:S(2)}) async-start(), calls=%async_computation.2 | async-start | bytes 37748736 | tf_op jit(solution)/shard_map/all_gather | solution.py:90
  26.7 0.7 copy-start.5
  26.7 2.1 copy-start.4
  40.3 94.4 %all-to-all-start = ((f32[32,32,1024]{2,1,0:T(8,128)}), f32[32,32,1024]{2,1,0:T(8,128)}, u32[]{:S(2)}, u32[]{:S(2)}) async-start(f32[32,32,1024]{2,1,0:T(8,128)} %select_select_fusion), calls=%async_computation | async-start | bytes 8388608 | tf_op jit(solution)/shard_map/all_to_all | solution.py:88
  265.6 218.9 %all-reduce.3.cloned.1.call-start = ((), (), s32[]{:S(2)}) async-start(), calls=%async_computation.1 | async-start | bytes 8388608 | tf_op jit(solution)/shard_map/psum | solution.py:91
  270.0 2.0 copy-start.3
  499.5 1.9 copy-start.2
  633.4 75.0 %copy-start.1 = (s32[1,128,128]{2,1,0:T(8,128)S(1)}, s32[1,128,128]{2,1,0:T(8,128)}, u32[]{:S(2)}) copy-start(s32[1,128,128]{2,1,0:T(8,128)} %param.10) | copy-start | bytes 196612
Sparse Core Ops, SparseCore 0:
  26.9 208.3 all-gather.2
  286.4 155.1 all-reduce.2
